TPU v7x, 512 devices: a whole 4x8x8 slice. The times are simulated.
512 devices in a mesh: pos: 64 (over z, y_lo, x), head: 8 (over y_hi, core).
Axes of the slice: x: 4, y: 8 (y_hi: 4, y_lo: 2; y = y_hi * 2 + y_lo), z: 8, core: 2. Of those that a mesh axis runs over, the one named last changes fastest.
Arguments:
- token_ids: int32 [65536], P('pos'), may hold values from 0 to 255
- token_table: float32 [256, 1024], replicated, may hold values from -6 to 6
- row_table: float32 [256, 1024], replicated, may hold values from -6 to 6
- col_table: float32 [256, 1024], replicated, may hold values from -6 to 6
- chan_table: float32 [3, 1024], replicated, may hold values from -6 to 6
- w_query: float32 [1024, 1024], P(None, 'head'), as said below
- w_key: float32 [1024, 1024], P(None, 'head'), as said below
- w_value: float32 [1024, 1024], P(None, 'head'), may hold values from -0.1875 to 0.1875
- w_out: float32 [1024, 1024], P('head', 'pos'), may hold values from -0.1875 to 0.1875
- w_in: float32 [1024, 4096], P('pos', 'head'), may hold values from -0.1875 to 0.1875
- w_down: float32 [4096, 1024], P('head', 'pos'), may hold values from -0.09375 to 0.09375
Outputs:
- latent_out: float32 [512, 1024], P('pos')
Inputs may be any that keep to these rules, and one draw needn't show every extreme that they name: `w_query`: entries of order 1024^-0.5 times a few. `w_key`: entries of order 1024^-0.5 times a few, or larger.
All inputs are finite; a program needn't handle non-finite values.
Results may differ from a plain program's by a relative error of at most 0.0003.
Values sent between devices are 32-bit elements; how exact they have to be, the bound alone decides.
No kernel may reach another device: no remote copies, remote signals or barrier semaphores. Data moves between devices by JAX's collectives and lax.ppermute only.
A program may use at most 128 MiB of HBM per device.

v0:
```python
import jax
import jax.numpy as jnp
from jax import lax
from jax.sharding import PartitionSpec as P

HD = 64
IMG = 256
LAT = 512


def broadcast(shard, axis, root):
    mine = lax.axis_index(axis) == root
    return lax.psum(jnp.where(mine, shard, jnp.zeros_like(shard)), axis)


def combined_all(value, axis, join):
    pieces = jax.tree.map(lambda part: lax.all_gather(part, axis), value)
    head = jax.tree.map(lambda part: part[0], pieces)
    tail = jax.tree.map(lambda part: part[1:], pieces)
    so_far, _ = lax.scan(lambda so_far, piece: (join(so_far, piece), None), head, tail)
    return so_far


def layer_norm(values):
    center = values - jnp.mean(values, axis=-1, keepdims=True)
    spread = jnp.mean(center * center, axis=-1, keepdims=True)
    return center * lax.rsqrt(spread + 1e-05)


def embed(ids, where, tables):
    token_table, row_table, col_table, chan_table = tables
    channel = where % 3
    pixel = where // 3
    summed = jnp.take(token_table, ids, axis=0) + jnp.take(row_table, pixel // IMG, axis=0)
    summed = (
        summed + jnp.take(col_table, pixel % IMG, axis=0) + jnp.take(chan_table, channel, axis=0)
    )
    return layer_norm(summed)


def merge_states(first, second):
    peak = jnp.maximum(first[0], second[0])
    left = jnp.exp(first[0] - peak)
    right = jnp.exp(second[0] - peak)
    weight = first[1] * left + second[1] * right
    accum = first[2] * left[..., None] + second[2] * right[..., None]
    return (peak, weight, accum)


def head_sum(partial_value):
    return lax.psum(partial_value, "head")


def per_device(
    token_ids,
    token_table,
    row_table,
    col_table,
    chan_table,
    w_query,
    w_key,
    w_value,
    w_out,
    w_in,
    w_down,
):
    highest = lax.Precision.HIGHEST
    tables = (token_table, row_table, col_table, chan_table)
    local = token_ids.shape[0]
    n_pos = lax.axis_size("pos")
    index = lax.axis_index("pos")
    total = local * n_pos
    heads_dev = w_key.shape[1] // HD
    key_block = min(512, local)
    lat_pos = total - LAT + jnp.arange(LAT)
    own_queries = jnp.dot(
        embed(token_ids[local - LAT :], lat_pos, tables), w_query, precision=highest
    )
    queries = broadcast(own_queries, "pos", n_pos - 1)
    queries = queries.reshape(LAT, heads_dev, HD).transpose(1, 0, 2) * HD ** (-0.5)

    def step(carry, start):
        top, weight, accum = carry
        where = index * local + start + jnp.arange(key_block)
        ids = lax.dynamic_slice_in_dim(token_ids, start, key_block)
        emb = embed(ids, where, tables)
        keys = jnp.dot(emb, w_key, precision=highest).reshape(key_block, heads_dev, HD)
        vals = jnp.dot(emb, w_value, precision=highest).reshape(key_block, heads_dev, HD)
        scores = jnp.einsum("hld,khd->hlk", queries, keys, precision=highest)
        scores = jnp.where(where[None, None, :] <= lat_pos[None, :, None], scores, -1e30)
        new_top = jnp.maximum(top, jnp.max(scores, axis=-1))
        factor = jnp.exp(top - new_top)
        probs = jnp.exp(scores - new_top[..., None])
        weight = weight * factor + jnp.sum(probs, axis=-1)
        accum = accum * factor[..., None] + jnp.einsum(
            "hlk,khd->hld", probs, vals, precision=highest
        )
        return ((new_top, weight, accum), None)

    starts = jnp.arange(local // key_block) * key_block
    init = (
        jnp.full((heads_dev, LAT), -1e30, jnp.float32),
        jnp.zeros((heads_dev, LAT), jnp.float32),
        jnp.zeros((heads_dev, LAT, HD), jnp.float32),
    )
    (top, weight, accum), _ = lax.scan(step, init, starts)
    lat_rows = LAT // n_pos
    top, weight, accum = combined_all((top, weight, accum), "pos", merge_states)
    weight = lax.dynamic_slice_in_dim(weight, index * lat_rows, lat_rows, 1)
    accum = lax.dynamic_slice_in_dim(accum, index * lat_rows, lat_rows, 1)
    attended = (accum / weight[..., None]).transpose(1, 0, 2).reshape(lat_rows, heads_dev * HD)
    whole_out, whole_in, whole_down = (
        lax.all_gather(w_out, "pos", axis=1, tiled=True),
        lax.all_gather(w_in, "pos", axis=0, tiled=True),
        lax.all_gather(w_down, "pos", axis=1, tiled=True),
    )
    projected = head_sum(jnp.dot(attended, whole_out, precision=highest))
    hidden = jax.nn.gelu(jnp.dot(layer_norm(projected), whole_in, precision=highest))
    return projected + head_sum(jnp.dot(hidden, whole_down, precision=highest))


def solution(mesh):
    placed = (
        P("pos"),
        P(),
        P(),
        P(),
        P(),
        P(None, "head"),
        P(None, "head"),
        P(None, "head"),
        P("head", "pos"),
        P("pos", "head"),
        P("head", "pos"),
    )
    return jax.shard_map(
        per_device, mesh=mesh, in_specs=placed, out_specs=P("pos", None), check_vma=False
    )
```

profile of v0, /device:TPU:2, one launch (start us, length us, event | category | flops | bytes accessed | tf_op | source)
XLA Modules:
  0.0 1644.0 jit_solution(15092672931124769)
XLA Ops:
  8.1 4.9 gather_fusion.4
  21.1 4.0 fusion.61
  26.8 4.3 fusion.34
  31.2 567.1 %all-reduce.2.cloned.1.call-done = f32[512,128]{1,0:T(8,128)} async-done(((f32[512,128]{1,0:T(8,128)}), f32[512,128]{1,0:T(8,128)}) %all-reduce.2.cloned.1.call-update) | async-done | bytes 262160 | tf_op jit(solution)/shard_map/psum | solution.py:13
  599.4 72.5 %while.33 = (s32[]{:T(128)}, f32[2,512]{1,0:T(2,128)S(1)}, f32[2,512]{1,0:T(2,128)S(1)}, f32[2,512,64]{1,2,0:T(8,128)}, s32[2]{0:T(128)S(1)}, /*index=5*/s32[]{:...) while((s32[]{:T(128)}, f32[2,512]{1,0:T(2,128)S(1)}, ...), condition=%wide.region_8.11_spmd.clone, body=%wide.region_3.0_spmd.clone.sunk | while | flops 2427988480 | bytes 55456068 | solution.py:106
  608.4 4.8 gather_fusion.1
  616.0 4.0 fusion.101
  621.0 3.2 fusion.107
  627.0 3.4 fusion.103
  644.1 4.8 gather_fusion.1
  651.7 4.0 fusion.101
  656.7 3.2 fusion.107
  662.7 3.4 fusion.103
  668.4 3.6 fusion.108
  673.3 155.9 %all_gather.33 = f32[128,1024]{0,1:T(8,128)S(1)} all-gather(f32[128,16]{0,1:T(8,128)S(1)} %copy-done.12), channel_id=1, replica_groups=mesh['pos'=64,'head'=8] {'pos'}, dimensions={1}, use_global_device_ids=true | all-gather | bytes 532480 | tf_op jit(solution)/shard_map/all_gather | solution.py:113
  829.2 153.3 %all-gather.4 = f32[64,2,512]{2,1,0:T(2,128)S(1)} all-gather(f32[1,2,512]{2,1,0:T(2,128)S(1)} %bitcast.83), channel_id=3, replica_groups=mesh['pos'=64,'head'=8] {'pos'}, dimensions={0}, use_global_device_ids=true | all-gather | bytes 266240 | tf_op jit(solution)/shard_map/all_gather | solution.py:17
  982.5 151.4 %all-gather.3 = f32[64,2,512]{2,1,0:T(2,128)S(1)} all-gather(f32[1,2,512]{2,1,0:T(2,128)S(1)} %bitcast.82), channel_id=2, replica_groups=mesh['pos'=64,'head'=8] {'pos'}, dimensions={0}, use_global_device_ids=true | all-gather | bytes 266240 | tf_op jit(solution)/shard_map/all_gather | solution.py:17
  1135.1 12.2 slice.59
  1147.3 106.7 %while.32 = (s32[]{:T(128)}, f32[2,512]{1,0:T(2,128)S(1)}, f32[2,512]{1,0:T(2,128)S(1)}, f32[2,512,64]{2,1,0:T(8,128)S(1)}, f32[63,2,512]{2,1,0:T(2,128)S(1)}, /...) while((s32[]{:T(128)}, f32[2,512]{1,0:T(2,128)S(1)}, f32[2,512]{1,0:T(2,128)S(1)}, ...), condition=%wide.region_10.13_spmd, body=%wide.region_9.12_spmd.sunk | while | flops 202754 | bytes 1876061 | solution.py:20
  1254.8 27.2 %psum.22 = f32[8,1024]{1,0:T(8,128)S(1)} all-reduce(f32[8,1024]{1,0:T(8,128)S(1)} %fusion.62), channel_id=1, replica_groups=mesh['pos'=64,'head'=8] {'head'}, use_global_device_ids=true, to_apply=%region_11.14 | all-reduce | flops 8192 | bytes 65536 | tf_op jit(solution)/shard_map/psum | solution.py:51
  1282.3 22.3 %all-gather.9.cloned.1.call-done = f32[1024,512]{1,0:T(8,128)} async-done(((f32[16,512]{1,0:T(8,128)}), f32[1024,512]{1,0:T(8,128)}) %all-gather.9.cloned.1.call-update) | async-done | bytes 2097168 | tf_op jit(solution)/shard_map/all_gather | solution.py:114
  1307.3 298.9 %all-gather.11.cloned.1.call-done = f32[512,1024]{0,1:T(8,128)} async-done(((f32[512,16]{0,1:T(8,128)}), f32[512,1024]{0,1:T(8,128)}) %all-gather.11.cloned.1.call-update) | async-done | bytes 2097168 | tf_op jit(solution)/shard_map/all_gather | solution.py:115
  1606.2 3.4 fusion.63
  1609.6 27.2 %psum.23 = f32[8,1024]{1,0:T(8,128)S(1)} all-reduce(f32[8,1024]{1,0:T(8,128)S(1)} %fusion.63), channel_id=1, replica_groups=mesh['pos'=64,'head'=8] {'head'}, use_global_device_ids=true, to_apply=%region_14.17 | all-reduce | flops 8192 | bytes 65536 | tf_op jit(solution)/shard_map/psum | solution.py:51
  (377 shorter events, 156.6 us)
Async XLA Ops:
  6.5 20.2 %copy-start = (f32[1024,128]{1,0:T(8,128)S(1)}, f32[1024,128]{1,0:T(8,128)}, u32[]{:S(2)}) copy-start(f32[1024,128]{1,0:T(8,128)} %param.24) | copy-start | bytes 1572868
  6.5 591.7 %all-reduce.2.cloned.1.call-start = ((), (), s32[]{:S(2)}) async-start(), calls=%async_computation | async-start | bytes 524288 | tf_op jit(solution)/shard_map/psum | solution.py:13
  8.1 5.0 copy-start.4
  13.1 2.7 copy-start.5
  15.8 2.7 copy-start.2
  25.0 1.3 copy-start.7
  26.7 572.6 %copy-start.3 = (f32[256,1024]{1,0:T(8,128)S(1)}, f32[256,1024]{1,0:T(8,128)}, u32[]{:S(2)}) copy-start(f32[256,1024]{1,0:T(8,128)} %param.20) | copy-start | bytes 3145732
  26.8 572.6 %copy-start.8 = (f32[1024,128]{1,0:T(8,128)S(1)}, f32[1024,128]{1,0:T(8,128)}, u32[]{:S(2)}) copy-start(f32[1024,128]{1,0:T(8,128)} %param.25) | copy-start | bytes 1572868
  26.8 572.6 %copy-start.11 = (s32[1024]{0:T(1024)S(1)}, s32[1024]{0:T(1024)}, u32[]{:S(2)}) copy-start(s32[1024]{0:T(1024)} %param.19) | copy-start | bytes 12292
  31.1 1102.9 %all-gather.13.cloned.1.call-start = ((), (), s32[]{:S(2)}) async-start(), calls=%async_computation.3 | async-start | bytes 17039360 | tf_op jit(solution)/shard_map/all_gather | solution.py:17
  599.4 73.9 %copy-start.12 = (f32[128,16]{0,1:T(8,128)S(1)}, f32[128,16]{0,1:T(8,128)}, u32[]{:S(2)}) copy-start(f32[128,16]{0,1:T(8,128)} %param.27) | copy-start | bytes 24580
  620.0 1.0 copy-start.9
  630.4 2.2 copy-start.10
  630.4 2.3 copy-start.6
  655.7 1.0 copy-start.9
  666.1 2.2 copy-start.10
  666.1 2.3 copy-start.6
  672.0 632.7 %all-gather.9.cloned.1.call-start = ((), (), s32[]{:S(2)}) async-start(), calls=%async_computation.1 | async-start | bytes 2129920 | tf_op jit(solution)/shard_map/all_gather | solution.py:114
  672.7 933.5 %all-gather.11.cloned.1.call-start = ((), (), s32[]{:S(2)}) async-start(), calls=%async_computation.2 | async-start | bytes 2129920 | tf_op jit(solution)/shard_map/all_gather | solution.py:115
  1282.3 355.2 %copy-start.1 = (f32[1024,128]{1,0:T(8,128)S(1)}, f32[1024,128]{1,0:T(8,128)}, u32[]{:S(2)}) copy-start(f32[1024,128]{1,0:T(8,128)} %param.24) | copy-start | bytes 1572868
Sparse Core Ops, SparseCore 0:
  31.2 567.0 all-reduce.1
  672.1 330.5 all-gather.12
  1004.8 299.7 all-gather.8
  1306.6 299.6 all-gather.10
where the time goes:
time: 1650 us; the launch traced here: 1640 us
  waiting for transfers between devices  890 us (54%)
  blocking collectives  515 us (31%)
  local copies, waits for them, and re-layouts  130 us (8%)
  other arithmetic  52.8 us (3%)
  matrix products  35.3 us (2%)
    psum x1, waiting for transfers between devices, broadcast(): return lax.psum(jnp.where(mine, shard, jnp.zeros_like(shard)), axis)  567 us
    all_gather x2, blocking collectives, combined_all(): pieces = jax.tree.map(lambda part: lax.all_gather(part, axis), value)  305 us
    all_gather x1, waiting for transfers between devices, per_device(): lax.all_gather(w_down, 'pos', axis=1, tiled=True)  299 us
    all_gather x1, blocking collectives, per_device(): lax.all_gather(w_out, 'pos', axis=1, tiled=True)  156 us
    dynamic_slice x126, local copies, waits for them, and re-layouts, combined_all(): lax.scan(lambda so_far, piece: (join(so_far, piece), None), head, tail)  73.7 us
    psum x2, blocking collectives, head_sum(): return lax.psum(partial_value, 'head')  54.4 us
  transfers between devices with their start and end apart: 4, of which 3 were waited for; matrix products, arithmetic and copies ran while one was open for 7% of the time, Pallas kernels for 0%

commit v1 on v0

--- a/solution.py
+++ b/solution.py
@@ -10,7 +10,7 @@
 
 def broadcast(shard, axis, root):
     mine = lax.axis_index(axis) == root
-    return lax.psum(jnp.where(mine, shard, jnp.zeros_like(shard)), axis)
+    return jnp.sum(lax.all_gather(jnp.where(mine, shard, jnp.zeros_like(shard)), axis), axis=0)
 
 
 def combined_all(value, axis, join):

time: 1650 us -> 1420 us (0.86)
  waiting for transfers between devices: 890 us -> 654 us
    psum x1 -> x0, waiting for transfers between devices: 567 us -> none  [broadcast(): return lax.psum(jnp.where(mine, shard, jnp.zeros_like(shard)), axis)]
    all_gather x0 -> x1, waiting for transfers between devices: none -> 335 us  [broadcast(): lax.all_gather(jnp.where(mine, shard, jnp.zeros_like(shard)), axis)]
  transfers between devices with their start and end apart: 4 -> 4, of which waited for: 3 -> 3; matrix products, arithmetic and copies ran while one was open for 7% -> 9% of each run, Pallas kernels for 0% -> 0%
where the time goes in v1:
time: 1420 us
  waiting for transfers between devices  654 us (46%)
  blocking collectives  517 us (36%)
  local copies, waits for them, and re-layouts  129 us (9%)
  other arithmetic  58.5 us (4%)
  matrix products  37.2 us (3%)
    all_gather x1, waiting for transfers between devices, broadcast(): lax.all_gather(jnp.where(mine, shard, jnp.zeros_like(shard)), axis)  335 us
    all_gather x2, blocking collectives, combined_all(): pieces = jax.tree.map(lambda part: lax.all_gather(part, axis), value)  308 us
    all_gather x1, waiting for transfers between devices, per_device(): lax.all_gather(w_down, 'pos', axis=1, tiled=True)  299 us
    all_gather x1, blocking collectives, per_device(): lax.all_gather(w_out, 'pos', axis=1, tiled=True)  154 us
    dynamic_slice x126, local copies, waits for them, and re-layouts, combined_all(): lax.scan(lambda so_far, piece: (join(so_far, piece), None), head, tail)  73.7 us
    psum x2, blocking collectives, head_sum(): return lax.psum(partial_value, 'head')  54.4 us
    add x63, other arithmetic, merge_states(): accum = first[2] * left[..., None] + second[2] * right[..., None]  29.1 us
  transfers between devices with their start and end apart: 4, of which 3 were waited for; matrix products, arithmetic and copies ran while one was open for 9% of the time, Pallas kernels for 0%

profile of v1, /device:TPU:2, one launch (start us, length us, event | category | flops | bytes accessed | tf_op | source)
XLA Modules:
  0.0 1416.9 jit_solution(8872194852928733295)
XLA Ops:
  8.1 4.9 gather_fusion.4
  21.1 4.0 fusion.61
  26.7 4.2 fusion.34
  31.0 334.8 %all-gather.15.cloned.1.call-done = f32[32768,128]{1,0:T(8,128)} async-done(((f32[512,128]{1,0:T(8,128)}), f32[32768,128]{1,0:T(8,128)}) %all-gather.15.cloned.1.call-update) | async-done | bytes 16777232 | tf_op jit(solution)/shard_map/all_gather | solution.py:13
  365.8 6.7 reduce_sum.86
  372.7 73.4 %while.33 = (s32[]{:T(128)}, f32[2,512]{1,0:T(2,128)S(1)}, f32[2,512]{1,0:T(2,128)S(1)}, f32[2,512,64]{1,2,0:T(8,128)}, s32[2]{0:T(128)S(1)}, /*index=5*/s32[]{:...) while((s32[]{:T(128)}, f32[2,512]{1,0:T(2,128)S(1)}, ...), condition=%wide.region_8.11_spmd.clone, body=%wide.region_3.0_spmd.clone.sunk | while | flops 2427988480 | bytes 53358888 | solution.py:106
  381.7 4.8 gather_fusion.1
  389.3 4.0 fusion.101
  393.7 4.3 fusion.107
  400.7 3.4 fusion.103
  417.8 4.8 gather_fusion.1
  425.4 4.0 fusion.101
  429.8 4.3 fusion.107
  442.5 3.5 fusion.108
  447.4 154.0 %all_gather.41 = f32[128,1024]{0,1:T(8,128)S(1)} all-gather(f32[128,16]{0,1:T(8,128)S(1)} %copy-done.11), channel_id=1, replica_groups=mesh['pos'=64,'head'=8] {'pos'}, dimensions={1}, use_global_device_ids=true | all-gather | bytes 532480 | tf_op jit(solution)/shard_map/all_gather | solution.py:113
  601.3 157.1 %all-gather.5 = f32[64,2,512]{2,1,0:T(2,128)S(1)} all-gather(f32[1,2,512]{2,1,0:T(2,128)S(1)} %bitcast.85), channel_id=4, replica_groups=mesh['pos'=64,'head'=8] {'pos'}, dimensions={0}, use_global_device_ids=true | all-gather | bytes 266240 | tf_op jit(solution)/shard_map/all_gather | solution.py:17
  758.5 151.2 %all-gather.4 = f32[64,2,512]{2,1,0:T(2,128)S(1)} all-gather(f32[1,2,512]{2,1,0:T(2,128)S(1)} %bitcast.84), channel_id=3, replica_groups=mesh['pos'=64,'head'=8] {'pos'}, dimensions={0}, use_global_device_ids=true | all-gather | bytes 266240 | tf_op jit(solution)/shard_map/all_gather | solution.py:17
  911.0 12.2 slice.59
  923.2 106.6 %while.32 = (s32[]{:T(128)}, f32[2,512]{1,0:T(2,128)S(1)}, f32[2,512]{1,0:T(2,128)S(1)}, f32[2,512,64]{2,1,0:T(8,128)S(1)}, f32[63,2,512]{2,1,0:T(2,128)S(1)}, /...) while((s32[]{:T(128)}, f32[2,512]{1,0:T(2,128)S(1)}, f32[2,512]{1,0:T(2,128)S(1)}, ...), condition=%wide.region_10.13_spmd, body=%wide.region_9.12_spmd.sunk | while | flops 202754 | bytes 1876061 | solution.py:20
  1030.6 27.2 %psum.14 = f32[8,1024]{1,0:T(8,128)S(1)} all-reduce(f32[8,1024]{1,0:T(8,128)S(1)} %fusion.62), channel_id=1, replica_groups=mesh['pos'=64,'head'=8] {'head'}, use_global_device_ids=true, to_apply=%region_11.14 | all-reduce | flops 8192 | bytes 65536 | tf_op jit(solution)/shard_map/psum | solution.py:51
  1058.2 19.6 %all-gather.11.cloned.1.call-done = f32[1024,512]{1,0:T(8,128)} async-done(((f32[16,512]{1,0:T(8,128)}), f32[1024,512]{1,0:T(8,128)}) %all-gather.11.cloned.1.call-update) | async-done | bytes 2097168 | tf_op jit(solution)/shard_map/all_gather | solution.py:114
  1080.5 298.7 %all-gather.13.cloned.1.call-done = f32[512,1024]{0,1:T(8,128)} async-done(((f32[512,16]{0,1:T(8,128)}), f32[512,1024]{0,1:T(8,128)}) %all-gather.13.cloned.1.call-update) | async-done | bytes 2097168 | tf_op jit(solution)/shard_map/all_gather | solution.py:115
  1379.1 3.4 fusion.63
  1382.5 27.2 %psum.15 = f32[8,1024]{1,0:T(8,128)S(1)} all-reduce(f32[8,1024]{1,0:T(8,128)S(1)} %fusion.63), channel_id=1, replica_groups=mesh['pos'=64,'head'=8] {'head'}, use_global_device_ids=true, to_apply=%region_14.17 | all-reduce | flops 8192 | bytes 65536 | tf_op jit(solution)/shard_map/psum | solution.py:51
  (374 shorter events, 157.6 us)
Async XLA Ops:
  6.5 20.2 %copy-start = (f32[1024,128]{1,0:T(8,128)S(1)}, f32[1024,128]{1,0:T(8,128)}, u32[]{:S(2)}) copy-start(f32[1024,128]{1,0:T(8,128)} %param.24) | copy-start | bytes 1572868
  6.5 359.3 %all-gather.15.cloned.1.call-start = ((), (), s32[]{:S(2)}) async-start(), calls=%async_computation.2 | async-start | bytes 17039360 | tf_op jit(solution)/shard_map/all_gather | solution.py:13
  8.1 5.0 copy-start.4
  13.1 2.7 copy-start.5
  15.8 2.7 copy-start.2
  25.0 1.3 copy-start.7
  30.9 878.9 %all-gather.17.cloned.1.call-start = ((), (), s32[]{:S(2)}) async-start(), calls=%async_computation.3 | async-start | bytes 17039360 | tf_op jit(solution)/shard_map/all_gather | solution.py:17
  365.8 6.8 copy-start.3
  365.8 6.8 copy-start.8
  365.8 6.8 copy-start.10
  372.7 74.7 %copy-start.11 = (f32[128,16]{0,1:T(8,128)S(1)}, f32[128,16]{0,1:T(8,128)}, u32[]{:S(2)}) copy-start(f32[128,16]{0,1:T(8,128)} %param.27) | copy-start | bytes 24580
  404.0 2.2 copy-start.9
  404.1 2.3 copy-start.6
  440.2 2.2 copy-start.9
  440.2 2.3 copy-start.6
  446.0 631.7 %all-gather.11.cloned.1.call-start = ((), (), s32[]{:S(2)}) async-start(), calls=%async_computation | async-start | bytes 2129920 | tf_op jit(solution)/shard_map/all_gather | solution.py:114
  446.8 932.3 %all-gather.13.cloned.1.call-start = ((), (), s32[]{:S(2)}) async-start(), calls=%async_computation.1 | async-start | bytes 2129920 | tf_op jit(solution)/shard_map/all_gather | solution.py:115
  1058.1 352.2 %copy-start.1 = (f32[1024,128]{1,0:T(8,128)S(1)}, f32[1024,128]{1,0:T(8,128)}, u32[]{:S(2)}) copy-start(f32[1024,128]{1,0:T(8,128)} %param.24) | copy-start | bytes 1572868
Sparse Core Ops, SparseCore 0:
  31.0 334.7 all-gather.14
  446.2 326.9 all-gather.16
  775.3 302.4 all-gather.10
  1079.7 299.3 all-gather.12
